TPU v7x, 32 devices: a whole 2x2x4 slice. The times are simulated.
32 devices in a mesh: dp: 4 (over y, core), table: 8 (over z, x).
Axes of the slice: x: 2, y: 2, z: 4, core: 2. Of those that a mesh axis runs over, the one named last changes fastest.
Arguments:
- table: float32 [131072, 256], P(('dp', 'table')), may hold values from -6 to 6
- hidden: float32 [16384, 256], P(('dp', 'table')), may hold values from -24 to 24
- neg_ids: int32 [4, 8, 4, 128], P('dp', 'table'), may hold values from 0 to 4095
- pos_ids: int32 [16384], P(('dp', 'table')), may hold values from 0 to 4095
- dloss: float32 [16384], P(('dp', 'table')), may hold values from -4 to 4
Outputs:
- row_loss: float32 [16384], P(('dp', 'table'))
- grad_hidden: float32 [16384, 256], P(('dp', 'table'))
- grad_table: float32 [131072, 256], P(('dp', 'table'))
All inputs are finite; a program needn't handle non-finite values.
Results may differ from a plain program's by a relative error of at most 0.0003.
Values sent between devices are 32-bit elements; how exact they have to be, the bound alone decides.
A program may use at most 192 MiB of HBM per device.

v0:
```python
import math
import jax
import jax.numpy as jnp
from jax import lax
from jax.sharding import PartitionSpec as P


def local(table, hidden, neg_ids, pos_ids, dloss):
    feat_width = hidden.shape[1]
    logit_scale = 3.0 / math.sqrt(feat_width)
    dp_peers = lax.axis_size("dp")
    table_index = lax.axis_index("table")
    local_ids = neg_ids[0, 0]
    per_peer = local_ids.shape[1]
    local_count = dp_peers * per_peer
    own_rows = hidden.shape[0]
    outgoing = table[local_ids.reshape(-1)].reshape(dp_peers, per_peer, feat_width)
    candidates = lax.all_to_all(outgoing, "dp", split_axis=0, concat_axis=0, tiled=True).reshape(
        local_count, feat_width
    )
    row_side = jnp.stack([pos_ids.astype(jnp.float32), dloss], axis=1)
    group_hidden, group_side = (
        lax.all_gather(hidden, "table", axis=0, tiled=True),
        lax.all_gather(row_side, "table", axis=0, tiled=True),
    )
    targets = group_side[:, 0].astype(jnp.int32)
    weights = group_side[:, 1]
    logits = logit_scale * lax.dot_general(
        group_hidden,
        candidates,
        (((1,), (1,)), ((), ())),
        precision=lax.Precision.HIGHEST,
        preferred_element_type=jnp.float32,
    )
    offsets = table_index * local_count + lax.iota(jnp.int32, local_count)
    target_hits = offsets[None, :] == targets[:, None]
    logit_part = jnp.sum(jnp.where(target_hits, logits, 0.0), axis=1)
    local_max = jnp.max(logits, axis=1)
    row_max = lax.pmax(local_max, "table")
    exponent = jnp.exp(logits - row_max[:, None])
    row_total, target_logit = lax.psum((jnp.sum(exponent, axis=1), logit_part), "table")
    group_loss = row_max + jnp.log(row_total) - target_logit
    row_loss = lax.dynamic_slice_in_dim(group_loss, table_index * own_rows, own_rows, 0)
    coefficient = (
        logit_scale
        * weights[:, None]
        * (exponent / row_total[:, None] - target_hits.astype(jnp.float32))
    )
    grad_hidden = lax.psum_scatter(
        jnp.dot(
            coefficient,
            candidates,
            precision=lax.Precision.HIGHEST,
            preferred_element_type=jnp.float32,
        ),
        "table",
        scatter_dimension=0,
        tiled=True,
    )
    cand_grad = lax.dot_general(
        coefficient,
        group_hidden,
        (((0,), (0,)), ((), ())),
        precision=lax.Precision.HIGHEST,
        preferred_element_type=jnp.float32,
    )
    returned = lax.all_to_all(
        cand_grad.reshape(dp_peers, per_peer, feat_width),
        "dp",
        split_axis=0,
        concat_axis=0,
        tiled=True,
    )
    grad_table = (
        jnp.zeros(table.shape, jnp.float32)
        .at[local_ids.reshape(-1)]
        .add(returned.reshape(local_count, feat_width))
    )
    return (row_loss, grad_hidden, grad_table)


def solution(mesh):
    in_specs = (
        P(("dp", "table"), None),
        P(("dp", "table"), None),
        P("dp", "table", None, None),
        P(("dp", "table")),
        P(("dp", "table")),
    )
    out_specs = (P(("dp", "table")), P(("dp", "table"), None), P(("dp", "table"), None))
    return jax.shard_map(local, mesh=mesh, in_specs=in_specs, out_specs=out_specs, check_vma=False)
```

profile of v0, /device:TPU:0, one launch (start us, length us, event | category | flops | bytes accessed | tf_op | source)
XLA Modules:
  0.0 280.4 jit_solution(1260502819999587651)
XLA Ops:
  7.2 0.0 all-gather.2.cloned.1.call-start
  7.2 0.7 all-gather.2.cloned.1.call-update
  7.9 0.7 compare_select_fusion.1
  8.6 4.4 %gather_fusion = f32[512,256]{1,0:T(8,128)} fusion(f32[4096,256]{1,0:T(8,128)} %param.5, s32[1024]{0:T(1024)S(1)} %pad_clamp_fusion), kind=kCustom, calls=%fused_computation | custom fusion | bytes 1050624 | tf_op jit(solution)/shard_map/gather | solution.py:17
  13.0 4.3 %all-to-all-start = ((f32[4,128,256]{2,1,0:T(8,128)}), f32[4,128,256]{2,1,0:T(8,128)S(1)}, u32[]{:S(2)}, u32[]{:S(2)}) async-start(f32[4,128,256]{2,1,0:T(8,128)} %bitcast.2), calls=%async_computation | async-start | bytes 1048576 | tf_op jit(solution)/shard_map/all_to_all | solution.py:18
  17.3 0.0 reduce-scatter.2.cloned.1.call-start
  17.3 0.7 convert_element_type.10
  18.0 0.7 pad_maximum_fusion
  18.7 32.5 %all_gather.7 = f32[4096,2]{0,1:T(2,128)S(1)} all-gather(f32[512,2]{0,1:T(2,128)S(1)} %pad_maximum_fusion), channel_id=1, replica_groups=mesh['dp'=4,'table'=8] {'table'}, dimensions={0}, use_global_device_ids=true | all-gather | bytes 36864 | tf_op jit(solution)/shard_map/all_gather | solution.py:24
  51.2 0.0 all-to-all-done
  51.2 34.7 %all-gather.2.cloned.1.call-done = f32[4096,256]{1,0:T(8,128)} async-done(((f32[512,256]{1,0:T(8,128)}), f32[4096,256]{1,0:T(8,128)}) %all-gather.2.cloned.1.call-update) | async-done | bytes 4194320 | tf_op jit(solution)/shard_map/all_gather | solution.py:23
  85.9 10.9 %multiply_reduce_fusion = (f32[4096]{0:T(1024)S(1)}, f32[512,4096]{1,0:T(8,128)}) fusion(f32[512,256]{1,0:T(8,128)S(1)} %bitcast.25, f32[4096,256]{1,0:T(8,128)} %all-gather.2.cloned.1.call-done), kind=kOutput, calls=%fused_computation.10 | convolution fusion | flops 6446641152 | bytes 13123584 | tf_op jit(solution)/shard_map/dot_general | solution.py:28
  96.8 34.7 %pmax.7 = f32[4096]{0:T(1024)S(1)} all-reduce(f32[4096]{0:T(1024)S(1)} %get-tuple-element.9), channel_id=1, replica_groups=mesh['dp'=4,'table'=8] {'table'}, use_global_device_ids=true, to_apply=%region_1.2 | all-reduce | flops 4096 | bytes 32768 | tf_op jit(solution)/shard_map/pmax | solution.py:39
  131.5 4.7 %fusion.4 = (f32[4096]{0:T(1024)S(1)}, f32[4096]{0:T(1024)S(1)}) fusion(f32[512,4096]{1,0:T(8,128)} %get-tuple-element.10, f32[4096]{0:T(1024)S(1)} %pmax.7, s32[4096]{0:T(1024)S(1)} %bitcast.28, s32[512]{0:T(512)S(1)} %iota_add_fusion), kind=kLoop, calls=%fused_computation.9 | loop fusion | flops 12574720 | bytes 8456192 | tf_op jit(solution)/shard_map/reduce_sum | solution.py:41
  136.2 33.2 %all-reduce = (f32[4096]{0:T(1024)S(1)}, f32[4096]{0:T(1024)S(1)}) all-reduce(f32[4096]{0:T(1024)S(1)} %get-tuple-element.4, f32[4096]{0:T(1024)S(1)} %get-tuple-element.3), channel_id=1, replica_groups=mesh['dp'=4,'table'=8] {'table'}, use_global_device_ids=true, to_apply=%region_5.6 | all-reduce | flops 8192 | bytes 65536 | tf_op jit(solution)/shard_map/psum | solution.py:41
  169.4 18.5 %fusion.9 = f32[4096,256]{1,0:T(8,128)} fusion(f32[512,256]{1,0:T(8,128)S(1)} %bitcast.26, f32[512,4096]{1,0:T(8,128)} %get-tuple-element.10, f32[4096]{0:T(1024)S(1)} %get-tuple-element.6, f32[4096]{0:T(1024)S(1)} %bitcast.31, s32[4096]{0:T(1024)S(1)} %bitcast.29, f32[4096]{0:T(1024)S(1)} %pmax.7, s32[512]{0:T(512)S(1)} %iota_add_fusion), kind=kOutput, calls=%fused_computation.23 | convolution fusion | flops 6457131008 | bytes 13174784 | tf_op jit(solution)/shard_map/dot_general | solution.py:50
  187.9 0.0 reduce-scatter.2.cloned.1.call-update
  187.9 14.0 %fusion.7 = f32[512,256]{1,0:T(8,128)} fusion(f32[4096,256]{1,0:T(8,128)} %all-gather.2.cloned.1.call-done, f32[512,4096]{1,0:T(8,128)} %get-tuple-element.10, f32[4096]{0:T(1024)S(1)} %get-tuple-element.6, f32[4096]{0:T(1024)S(1)} %bitcast.32, s32[4096]{0:T(1024)S(1)} %bitcast.30, f32[4096]{0:T(1024)S(1)} %pmax.7, s32[512]{0:T(512)S(1)} %iota_add_fusion), kind=kOutput, calls=%fused_computation.22 | convolution fusion | flops 6457131008 | bytes 13174784 | tf_op jit(solution)/shard_map/dot_general | solution.py:60
  202.0 3.5 %all-to-all-start.1 = ((f32[4,128,256]{2,1,0:T(8,128)}), f32[4,128,256]{2,1,0:T(8,128)S(1)}, u32[]{:S(2)}, u32[]{:S(2)}) async-start(f32[4,128,256]{2,1,0:T(8,128)} %bitcast.9), calls=%async_computation.2 | async-start | bytes 1048576 | tf_op jit(solution)/shard_map/all_to_all | solution.py:67
  205.4 0.7 dynamic-slice_subtract_fusion
  206.1 8.1 %all-to-all-done.1 = f32[4,128,256]{2,1,0:T(8,128)S(1)} async-done(((f32[4,128,256]{2,1,0:T(8,128)}), f32[4,128,256]{2,1,0:T(8,128)S(1)}, u32[]{:S(2)}, u32[]{:S(2)}) %all-to-all-start.1) | async-done | bytes 524320 | tf_op jit(solution)/shard_map/all_to_all | solution.py:67
  214.2 5.5 %scatter_custom_fusion = f32[4096,256]{1,0:T(8,128)} fusion(s32[512]{0:T(512)S(1)} %bitcast.34, f32[512,256]{1,0:T(8,128)S(1)} %bitcast.27, f32[]{:T(128)} %constant.11.clone.1), kind=kCustom, calls=%fused_computation.11 | custom fusion | flops 131072 | bytes 4194308 | tf_op jit(solution)/shard_map/scatter-add | solution.py:77
  219.8 53.8 %reduce-scatter.2.cloned.1.call-done = f32[512,256]{1,0:T(8,128)} async-done(((f32[4096,256]{1,0:T(8,128)}), f32[512,256]{1,0:T(8,128)}) %reduce-scatter.2.cloned.1.call-update) | async-done | bytes 524304 | tf_op jit(solution)/shard_map/reduce_scatter | solution.py:49
  (3 shorter events, 0.0 us)
Async XLA Ops:
  7.2 78.7 %all-gather.2.cloned.1.call-start = ((), (), s32[]{:S(2)}) async-start(), calls=%async_computation.3 | async-start | bytes 4718592 | tf_op jit(solution)/shard_map/all_gather | solution.py:23
  13.0 38.2 %all-to-all-start = ((f32[4,128,256]{2,1,0:T(8,128)}), f32[4,128,256]{2,1,0:T(8,128)S(1)}, u32[]{:S(2)}, u32[]{:S(2)}) async-start(f32[4,128,256]{2,1,0:T(8,128)} %bitcast.2), calls=%async_computation | async-start | bytes 1048576 | tf_op jit(solution)/shard_map/all_to_all | solution.py:18
  17.3 256.3 %reduce-scatter.2.cloned.1.call-start = ((), (), s32[]{:S(2)}) async-start(), calls=%async_computation.4 | async-start | bytes 4718592 | tf_op jit(solution)/shard_map/reduce_scatter | solution.py:49
  202.0 12.3 %all-to-all-start.1 = ((f32[4,128,256]{2,1,0:T(8,128)}), f32[4,128,256]{2,1,0:T(8,128)S(1)}, u32[]{:S(2)}, u32[]{:S(2)}) async-start(f32[4,128,256]{2,1,0:T(8,128)} %bitcast.9), calls=%async_computation.2 | async-start | bytes 1048576 | tf_op jit(solution)/shard_map/all_to_all | solution.py:67
Sparse Core Ops, SparseCore 0:
  10.1 75.7 all-gather.1
  188.0 85.4 reduce-scatter.1
where the time goes:
time: 281 us; the launch traced here: 280 us
  blocking collectives  100 us (36%)
  waiting for transfers between devices  97.3 us (35%)
  matrix products  43.4 us (15%)
  between operations  14.1 us (5%)
  other arithmetic  13 us (5%)
  starting transfers between devices  7.78 us (3%)
  local copies, waits for them, and re-layouts  4.42 us (2%)
    reduce_scatter x1, waiting for transfers between devices, local(): lax.psum_scatter(jnp.dot(coefficient, candidates, precision=lax.Precision...  53.8 us
    pmax x1, blocking collectives, local(): row_max = lax.pmax(local_max, 'table')  34.7 us
    all_gather x1, waiting for transfers between devices, local(): lax.all_gather(hidden, 'table', axis=0, tiled=True)  34.7 us
    psum x1, blocking collectives, local(): lax.psum((jnp.sum(exponent, axis=1), logit_part), 'table')  33.2 us
    all_gather x1, blocking collectives, local(): lax.all_gather(row_side, 'table', axis=0, tiled=True)  32.5 us
    dot_general x1, matrix products, local(): jnp.dot(coefficient, candidates, precision=lax.Precision.HIGHEST, preferr...  18.5 us
    dot_general x1, matrix products, local(): lax.dot_general(coefficient, group_hidden, (((0,), (0,)), ((), ())), prec...  14 us
    dot_general x1, matrix products, local(): lax.dot_general(group_hidden, candidates, (((1,), (1,)), ((), ())), preci...  10.9 us
  transfers between devices with their start and end apart: 4, of which 3 were waited for; matrix products, arithmetic and copies ran while one was open for 10% of the time, Pallas kernels for 0%

commit v1 on v0

--- a/solution.py
+++ b/solution.py
@@ -19,9 +19,18 @@
         local_count, feat_width
     )
     row_side = jnp.stack([pos_ids.astype(jnp.float32), dloss], axis=1)
+    settle_the_surface = lambda a0: jnp.concatenate(
+        lax.all_to_all(
+            jnp.stack([a0 for _ in range(lax.psum(1, axis_name="table"))]),
+            "table",
+            concat_axis=0,
+            split_axis=0,
+        ),
+        axis=0,
+    )
     group_hidden, group_side = (
         lax.all_gather(hidden, "table", axis=0, tiled=True),
-        lax.all_gather(row_side, "table", axis=0, tiled=True),
+        settle_the_surface(row_side),
     )
     targets = group_side[:, 0].astype(jnp.int32)
     weights = group_side[:, 1]

time: 281 us -> 281 us (level)
  blocking collectives: 100 us -> 67.9 us
  waiting for transfers between devices: 97.3 us -> 122 us
  starting transfers between devices: 7.78 us -> 14.3 us
    all_gather x1 -> x0, blocking collectives: 32.5 us -> none  [local(): lax.all_gather(row_side, 'table', axis=0, tiled=True)]
    all_gather x1, waiting for transfers between devices: 34.7 us -> 49.4 us  [local(): lax.all_gather(hidden, 'table', axis=0, tiled=True)]
    all_to_all x1, waiting for transfers between devices: 0.01 us -> 8.69 us  [local(): lax.all_to_all(outgoing, 'dp', split_axis=0, concat_axis=0, tiled=True)]
    all_to_all x0 -> x1, starting transfers between devices: none -> 7.28 us  [local(): lax.all_to_all(jnp.stack([a0 for _ in range(lax.psum(1, axis_name='table'...]
  transfers between devices with their start and end apart: 4 -> 5, of which waited for: 3 -> 5; matrix products, arithmetic and copies ran while one was open for 10% -> 10% of each run, Pallas kernels for 0% -> 0%
where the time goes in v1:
time: 281 us; the launch traced here: 280 us
  waiting for transfers between devices  122 us (43%)
  blocking collectives  67.9 us (24%)
  matrix products  43.4 us (15%)
  starting transfers between devices  14.3 us (5%)
  between operations  14.1 us (5%)
  other arithmetic  13 us (5%)
  local copies, waits for them, and re-layouts  5.11 us (2%)
    reduce_scatter x1, waiting for transfers between devices, local(): lax.psum_scatter(jnp.dot(coefficient, candidates, precision=lax.Precision...  53.8 us
    all_gather x1, waiting for transfers between devices, local(): lax.all_gather(hidden, 'table', axis=0, tiled=True)  49.4 us
    pmax x1, blocking collectives, local(): row_max = lax.pmax(local_max, 'table')  34.7 us
    psum x1, blocking collectives, local(): lax.psum((jnp.sum(exponent, axis=1), logit_part), 'table')  33.2 us
    dot_general x1, matrix products, local(): jnp.dot(coefficient, candidates, precision=lax.Precision.HIGHEST, preferr...  18.5 us
    dot_general x1, matrix products, local(): lax.dot_general(coefficient, group_hidden, (((0,), (0,)), ((), ())), prec...  14 us
    dot_general x1, matrix products, local(): lax.dot_general(group_hidden, candidates, (((1,), (1,)), ((), ())), preci...  10.9 us
    all_to_all x1, waiting for transfers between devices, local(): lax.all_to_all(outgoing, 'dp', split_axis=0, concat_axis=0, tiled=True)  8.69 us
  transfers between devices with their start and end apart: 5, of which 5 were waited for; matrix products, arithmetic and copies ran while one was open for 10% of the time, Pallas kernels for 0%

profile of v1, /device:TPU:0, one launch (start us, length us, event | category | flops | bytes accessed | tf_op | source)
XLA Modules:
  0.0 280.2 jit_solution(136171443852796749)
XLA Ops:
  7.2 0.0 all-gather.2.cloned.1.call-start
  7.2 0.7 all-gather.2.cloned.1.call-update
  7.9 0.7 convert_element_type.10
  8.6 0.7 pad_maximum_fusion
  9.3 0.6 stack.11
  9.9 7.3 %all-to-all-start.1 = ((f32[8,512,2]{1,2,0:T(2,128)}), f32[8,512,2]{1,2,0:T(2,128)S(1)}, u32[]{:S(2)}, u32[]{:S(2)}) async-start(f32[8,512,2]{1,2,0:T(2,128)} %stack.11), calls=%async_computation.1 | async-start | bytes 65536 | tf_op jit(solution)/shard_map/all_to_all | solution.py:23
  17.2 0.7 compare_select_fusion.1
  17.9 4.5 %gather_fusion = f32[512,256]{1,0:T(8,128)} fusion(f32[4096,256]{1,0:T(8,128)} %param.5, s32[1024]{0:T(1024)S(1)} %pad_clamp_fusion), kind=kCustom, calls=%fused_computation | custom fusion | bytes 1050624 | tf_op jit(solution)/shard_map/gather | solution.py:17
  22.4 1.6 all-to-all-done.1
  24.0 3.5 %all-to-all-start = ((f32[4,128,256]{2,1,0:T(8,128)}), f32[4,128,256]{2,1,0:T(8,128)S(1)}, u32[]{:S(2)}, u32[]{:S(2)}) async-start(f32[4,128,256]{2,1,0:T(8,128)} %bitcast.2), calls=%async_computation | async-start | bytes 1048576 | tf_op jit(solution)/shard_map/all_to_all | solution.py:18
  27.5 0.0 reduce-scatter.2.cloned.1.call-start
  27.5 8.7 %all-to-all-done = f32[4,128,256]{2,1,0:T(8,128)S(1)} async-done(((f32[4,128,256]{2,1,0:T(8,128)}), f32[4,128,256]{2,1,0:T(8,128)S(1)}, u32[]{:S(2)}, u32[]{:S(2)}) %all-to-all-start) | async-done | bytes 524320 | tf_op jit(solution)/shard_map/all_to_all | solution.py:18
  36.2 49.4 %all-gather.2.cloned.1.call-done = f32[4096,256]{1,0:T(8,128)} async-done(((f32[512,256]{1,0:T(8,128)}), f32[4096,256]{1,0:T(8,128)}) %all-gather.2.cloned.1.call-update) | async-done | bytes 4194320 | tf_op jit(solution)/shard_map/all_gather | solution.py:32
  85.6 10.9 %multiply_reduce_fusion = (f32[4096]{0:T(1024)S(1)}, f32[512,4096]{1,0:T(8,128)}) fusion(f32[512,256]{1,0:T(8,128)S(1)} %bitcast.26, f32[4096,256]{1,0:T(8,128)} %all-gather.2.cloned.1.call-done), kind=kOutput, calls=%fused_computation.10 | convolution fusion | flops 6446641152 | bytes 13123584 | tf_op jit(solution)/shard_map/dot_general | solution.py:37
  96.6 34.7 %pmax.7 = f32[4096]{0:T(1024)S(1)} all-reduce(f32[4096]{0:T(1024)S(1)} %get-tuple-element.9), channel_id=1, replica_groups=mesh['dp'=4,'table'=8] {'table'}, use_global_device_ids=true, to_apply=%region_1.2 | all-reduce | flops 4096 | bytes 32768 | tf_op jit(solution)/shard_map/pmax | solution.py:48
  131.3 4.7 %fusion.4 = (f32[4096]{0:T(1024)S(1)}, f32[4096]{0:T(1024)S(1)}) fusion(f32[512,4096]{1,0:T(8,128)} %get-tuple-element.10, f32[4096]{0:T(1024)S(1)} %pmax.7, s32[4096]{0:T(1024)S(1)} %bitcast.30, s32[512]{0:T(512)S(1)} %iota_add_fusion), kind=kLoop, calls=%fused_computation.9 | loop fusion | flops 12574720 | bytes 8456192 | tf_op jit(solution)/shard_map/reduce_sum | solution.py:50
  135.9 33.2 %all-reduce = (f32[4096]{0:T(1024)S(1)}, f32[4096]{0:T(1024)S(1)}) all-reduce(f32[4096]{0:T(1024)S(1)} %get-tuple-element.4, f32[4096]{0:T(1024)S(1)} %get-tuple-element.3), channel_id=1, replica_groups=mesh['dp'=4,'table'=8] {'table'}, use_global_device_ids=true, to_apply=%region_5.6 | all-reduce | flops 8192 | bytes 65536 | tf_op jit(solution)/shard_map/psum | solution.py:50
  169.2 18.5 %fusion.9 = f32[4096,256]{1,0:T(8,128)} fusion(f32[512,256]{1,0:T(8,128)S(1)} %bitcast.27, f32[512,4096]{1,0:T(8,128)} %get-tuple-element.10, f32[4096]{0:T(1024)S(1)} %get-tuple-element.6, f32[4096]{0:T(1024)S(1)} %bitcast.33, s32[4096]{0:T(1024)S(1)} %bitcast.31, f32[4096]{0:T(1024)S(1)} %pmax.7, s32[512]{0:T(512)S(1)} %iota_add_fusion), kind=kOutput, calls=%fused_computation.23 | convolution fusion | flops 6457131008 | bytes 13174784 | tf_op jit(solution)/shard_map/dot_general | solution.py:59
  187.6 0.0 reduce-scatter.2.cloned.1.call-update
  187.7 14.0 %fusion.7 = f32[512,256]{1,0:T(8,128)} fusion(f32[4096,256]{1,0:T(8,128)} %all-gather.2.cloned.1.call-done, f32[512,4096]{1,0:T(8,128)} %get-tuple-element.10, f32[4096]{0:T(1024)S(1)} %get-tuple-element.6, f32[4096]{0:T(1024)S(1)} %bitcast.34, s32[4096]{0:T(1024)S(1)} %bitcast.32, f32[4096]{0:T(1024)S(1)} %pmax.7, s32[512]{0:T(512)S(1)} %iota_add_fusion), kind=kOutput, calls=%fused_computation.22 | convolution fusion | flops 6457131008 | bytes 13174784 | tf_op jit(solution)/shard_map/dot_general | solution.py:69
  201.7 3.5 %all-to-all-start.2 = ((f32[4,128,256]{2,1,0:T(8,128)}), f32[4,128,256]{2,1,0:T(8,128)S(1)}, u32[]{:S(2)}, u32[]{:S(2)}) async-start(f32[4,128,256]{2,1,0:T(8,128)} %bitcast.10), calls=%async_computation.3 | async-start | bytes 1048576 | tf_op jit(solution)/shard_map/all_to_all | solution.py:76
  205.2 0.7 dynamic-slice_subtract_fusion
  205.9 8.1 %all-to-all-done.2 = f32[4,128,256]{2,1,0:T(8,128)S(1)} async-done(((f32[4,128,256]{2,1,0:T(8,128)}), f32[4,128,256]{2,1,0:T(8,128)S(1)}, u32[]{:S(2)}, u32[]{:S(2)}) %all-to-all-start.2) | async-done | bytes 524320 | tf_op jit(solution)/shard_map/all_to_all | solution.py:76
  214.0 5.5 %scatter_custom_fusion = f32[4096,256]{1,0:T(8,128)} fusion(s32[512]{0:T(512)S(1)} %bitcast.36, f32[512,256]{1,0:T(8,128)S(1)} %bitcast.28, f32[]{:T(128)} %constant.11.clone.1), kind=kCustom, calls=%fused_computation.11 | custom fusion | flops 131072 | bytes 4194308 | tf_op jit(solution)/shard_map/scatter-add | solution.py:86
  219.5 53.8 %reduce-scatter.2.cloned.1.call-done = f32[512,256]{1,0:T(8,128)} async-done(((f32[4096,256]{1,0:T(8,128)}), f32[512,256]{1,0:T(8,128)}) %reduce-scatter.2.cloned.1.call-update) | async-done | bytes 524304 | tf_op jit(solution)/shard_map/reduce_scatter | solution.py:58
  (3 shorter events, 0.0 us)
Async XLA Ops:
  7.2 78.5 %all-gather.2.cloned.1.call-start = ((), (), s32[]{:S(2)}) async-start(), calls=%async_computation.4 | async-start | bytes 4718592 | tf_op jit(solution)/shard_map/all_gather | solution.py:32
  9.9 14.1 %all-to-all-start.1 = ((f32[8,512,2]{1,2,0:T(2,128)}), f32[8,512,2]{1,2,0:T(2,128)S(1)}, u32[]{:S(2)}, u32[]{:S(2)}) async-start(f32[8,512,2]{1,2,0:T(2,128)} %stack.11), calls=%async_computation.1 | async-start | bytes 65536 | tf_op jit(solution)/shard_map/all_to_all | solution.py:23
  24.0 12.3 %all-to-all-start = ((f32[4,128,256]{2,1,0:T(8,128)}), f32[4,128,256]{2,1,0:T(8,128)S(1)}, u32[]{:S(2)}, u32[]{:S(2)}) async-start(f32[4,128,256]{2,1,0:T(8,128)} %bitcast.2), calls=%async_computation | async-start | bytes 1048576 | tf_op jit(solution)/shard_map/all_to_all | solution.py:18
  27.5 245.9 %reduce-scatter.2.cloned.1.call-start = ((), (), s32[]{:S(2)}) async-start(), calls=%async_computation.5 | async-start | bytes 4718592 | tf_op jit(solution)/shard_map/reduce_scatter | solution.py:58
  201.7 12.3 %all-to-all-start.2 = ((f32[4,128,256]{2,1,0:T(8,128)}), f32[4,128,256]{2,1,0:T(8,128)S(1)}, u32[]{:S(2)}, u32[]{:S(2)}) async-start(f32[4,128,256]{2,1,0:T(8,128)} %bitcast.10), calls=%async_computation.3 | async-start | bytes 1048576 | tf_op jit(solution)/shard_map/all_to_all | solution.py:76
Sparse Core Ops, SparseCore 0:
  10.1 75.4 all-gather.1
  187.8 85.5 reduce-scatter.1
